TPU v7x, 32 devices: a whole 2x2x4 slice. The times are simulated.
32 devices in a mesh: dp: 2 (over x), tensor: 4 (over z), fsdp: 4 (over y, core).
Axes of the slice: x: 2, y: 2, z: 4, core: 2. Of those that a mesh axis runs over, the one named last changes fastest.
Arguments:
- train_acts: bfloat16 [2048, 4096], P(('dp', 'fsdp'), 'tensor'), may hold values from -6 to 6
- val_acts: bfloat16 [2048, 4096], P(('dp', 'fsdp'), 'tensor'), may hold values from -6 to 6
- train_cot: bfloat16 [2048, 4096], P(('dp', 'fsdp'), 'tensor'), may hold values from -6 to 6
- val_cot: bfloat16 [2048, 4096], P(('dp', 'fsdp'), 'tensor'), may hold values from -6 to 6
- train_lengths: int32 [32], P(('dp', 'fsdp')), may hold values from 16 to 64
- val_lengths: int32 [32], P(('dp', 'fsdp')), may hold values from 16 to 64
- gate_weight: bfloat16 [4096, 11008], P(('dp', 'fsdp'), 'tensor'), may hold values from -0.09375 to 0.09375
- up_weight: bfloat16 [4096, 11008], P(('dp', 'fsdp'), 'tensor'), may hold values from -0.09375 to 0.09375
- in_basis: bfloat16 [11008, 64], P('tensor'), may hold values from -0.0546875 to 0.0546875
- out_basis: bfloat16 [4096, 128], P('tensor'), may hold values from -0.09375 to 0.09375
Outputs:
- scores: float32 [32, 32], P(('dp', 'fsdp'))
Inputs may be any that keep to these rules, and one draw needn't show every extreme that they name: `train_lengths`: an example's first length slots hold its tokens, the rest are padding. `val_lengths`: as for the training examples.
All inputs are finite; a program needn't handle non-finite values.
Results may differ from a plain program's by a relative error of at most 0.004.
Values may be sent and summed in bfloat16 or wider, within the bound.
No kernel may reach another device: no remote copies, remote signals or barrier semaphores. Data moves between devices by JAX's collectives and lax.ppermute only.
A program may use at most 128 MiB of HBM per device.

v0:
```python
import jax
import jax.numpy as jnp
from jax import lax
from jax.sharding import PartitionSpec as P

SEQ = 64


def outer_sums(in_proj, out_proj, valid):
    in_three = in_proj.reshape(valid.shape[0], valid.shape[1], in_proj.shape[1]) * valid[:, :, None]
    out_three = out_proj.reshape(valid.shape[0], valid.shape[1], out_proj.shape[1])
    return jnp.einsum("esj,esk->ejk", in_three, out_three, precision=lax.Precision.HIGHEST)


def on_device(
    train_acts,
    val_acts,
    train_cot,
    val_cot,
    train_lengths,
    val_lengths,
    gate_weight,
    up_weight,
    in_basis,
    out_basis,
):
    train_full, val_full = (
        lax.all_gather(train_acts, "tensor", axis=1, tiled=True),
        lax.all_gather(val_acts, "tensor", axis=1, tiled=True),
    )
    activations = jnp.concatenate([train_full, val_full], axis=0)
    cotangents = jnp.concatenate([train_cot, val_cot], axis=0)
    gate_sum = jnp.dot(
        activations,
        lax.all_gather(gate_weight, ("dp", "fsdp"), axis=0, tiled=True),
        preferred_element_type=jnp.float32,
    )
    up_sum = jnp.dot(
        activations,
        lax.all_gather(up_weight, ("dp", "fsdp"), axis=0, tiled=True),
        preferred_element_type=jnp.float32,
    )
    hidden = (jax.nn.silu(gate_sum) * up_sum).astype(jnp.bfloat16)
    in_part = jnp.dot(hidden, in_basis, preferred_element_type=jnp.float32)
    out_part = jnp.dot(cotangents, out_basis, preferred_element_type=jnp.float32)
    lengths = jnp.concatenate([train_lengths, val_lengths], axis=0)
    valid = (jnp.arange(SEQ, dtype=jnp.int32)[None, :] < lengths[:, None]).astype(jnp.float32)
    in_proj, out_proj = lax.psum((in_part, out_part), "tensor")
    sketch = outer_sums(in_proj, out_proj, valid)
    flat_sketch = sketch.reshape(sketch.shape[0], sketch.shape[1] * sketch.shape[2])
    unit_rows = flat_sketch * lax.rsqrt(
        jnp.sum(flat_sketch * flat_sketch, axis=1, keepdims=True) + 1e-06
    )
    train_count = train_lengths.shape[0]
    train_unit = unit_rows[:train_count]
    val_local = unit_rows[train_count:]
    width_all = flat_sketch.shape[1]
    share = width_all // lax.axis_size("tensor")
    first = lax.axis_index("tensor") * share
    train_share = lax.dynamic_slice_in_dim(train_unit, first, share, 1)
    val_share_local = lax.dynamic_slice_in_dim(val_local, first, share, 1)
    val_share = lax.all_gather(val_share_local, ("dp", "fsdp"), axis=0, tiled=True)
    partial_scores = jnp.dot(
        train_share,
        val_share.T,
        precision=lax.Precision.HIGHEST,
        preferred_element_type=jnp.float32,
    )
    product = lax.psum(partial_scores, "tensor")
    return product * jnp.sqrt(jnp.float32(width_all))


def solution(mesh):
    placed = (
        P(("dp", "fsdp"), "tensor"),
        P(("dp", "fsdp"), "tensor"),
        P(("dp", "fsdp"), "tensor"),
        P(("dp", "fsdp"), "tensor"),
        P(("dp", "fsdp")),
        P(("dp", "fsdp")),
        P(("dp", "fsdp"), "tensor"),
        P(("dp", "fsdp"), "tensor"),
        P("tensor", None),
        P("tensor", None),
    )
    return jax.shard_map(
        on_device, mesh=mesh, in_specs=placed, out_specs=P(("dp", "fsdp"), None), check_vma=False
    )
```

profile of v0, /device:TPU:0, one launch (start us, length us, event | category | flops | bytes accessed | tf_op | source)
XLA Modules:
  0.0 431.9 jit_solution(13203272675145067068)
XLA Ops:
  6.5 0.0 copy-start
  6.5 0.0 all-gather.6.cloned.1.call-start
  6.6 0.7 all-gather.6.cloned.1.call-update
  7.3 0.0 all-gather.8.cloned.1.call-start
  7.3 0.7 all-gather.8.cloned.1.call-update
  8.0 0.0 all-gather.10.cloned.1.call-start
  8.1 0.7 all-gather.10.cloned.1.call-update
  8.8 0.0 all-gather.12.cloned.1.call-start
  8.8 0.5 all-gather.12.cloned.1.call-update
  9.3 0.0 all-reduce.3.cloned.1.call-start
  9.4 1.1 fusion.1
  10.6 46.8 %all-gather.6.cloned.1.call-done = bf16[256,4096]{1,0:T(8,128)(2,1)} async-done(((bf16[256,1024]{1,0:T(8,128)(2,1)}), bf16[256,4096]{1,0:T(8,128)(2,1)}) %all-gather.6.cloned.1.call-update) | async-done | bytes 2097168 | tf_op jit(solution)/shard_map/all_gather | solution.py:28
  57.3 3.1 constant_dynamic-update-slice_fusion.1
  60.4 42.9 %all-gather.8.cloned.1.call-done = bf16[256,4096]{1,0:T(8,128)(2,1)} async-done(((bf16[256,1024]{1,0:T(8,128)(2,1)}), bf16[256,4096]{1,0:T(8,128)(2,1)}) %all-gather.8.cloned.1.call-update) | async-done | bytes 2097168 | tf_op jit(solution)/shard_map/all_gather | solution.py:29
  103.4 3.1 constant_dynamic-update-slice_fusion
  106.5 116.1 %all-gather.10.cloned.1.call-done = bf16[4096,2752]{0,1:T(8,128)(2,1)} async-done(((bf16[512,2752]{0,1:T(8,128)(2,1)}), bf16[4096,2752]{0,1:T(8,128)(2,1)}) %all-gather.10.cloned.1.call-update) | async-done | bytes 22544400 | tf_op jit(solution)/shard_map/all_gather | solution.py:35
  222.7 19.2 %fusion.15 = f32[512,2752]{0,1:T(8,128)} fusion(bf16[512,4096]{1,0:T(8,128)(2,1)} %constant_dynamic-update-slice_fusion, bf16[4096,2752]{0,1:T(8,128)(2,1)} %all-gather.10.cloned.1.call-done), kind=kOutput, calls=%fused_computation.25 | convolution fusion | flops 11542724608 | bytes 32374784 | tf_op jit(solution)/shard_map/dot_general | solution.py:33
  241.9 101.1 %all-gather.12.cloned.1.call-done = bf16[4096,2752]{0,1:T(8,128)(2,1)} async-done(((bf16[512,2752]{0,1:T(8,128)(2,1)}), bf16[4096,2752]{0,1:T(8,128)(2,1)}) %all-gather.12.cloned.1.call-update) | async-done | bytes 22544400 | tf_op jit(solution)/shard_map/all_gather | solution.py:40
  343.0 20.0 %fusion = f32[512,64]{0,1:T(8,128)S(1)} fusion(bf16[2752,64]{0,1:T(8,128)(2,1)S(1)} %copy-done, f32[512,2752]{0,1:T(8,128)} %fusion.15, bf16[512,4096]{1,0:T(8,128)(2,1)} %constant_dynamic-update-slice_fusion, bf16[4096,2752]{0,1:T(8,128)(2,1)} %all-gather.12.cloned.1.call-done), kind=kOutput, calls=%fused_computation.1 | convolution fusion | flops 11731533824 | bytes 32858112 | tf_op jit(solution)/shard_map/dot_general | solution.py:44
  363.1 0.1 reshape.37
  363.2 0.8 copy.12
  363.9 0.0 all-reduce.3.cloned.1.call-update
  364.0 0.1 pad_add_fusion
  364.0 0.1 fusion.10
  364.1 38.7 %all-reduce.3.cloned.1.call-done = (f32[8,64,128]{2,1,0:T(8,128)}, f32[8,64,64]{1,2,0:T(8,128)}) async-done(((f32[8,64,128]{2,1,0:T(8,128)}, f32[8,64,64]{1,2,0:T(8,128)}), (f32[8,64,128]{2,1,0:T(8,128)}, f32[8,64,64]{1,2,0:T(8,128)})) %all-reduce.3.cloned.1.call-update) | async-done | bytes 393232 | tf_op jit(solution)/shard_map/psum | solution.py:48
  402.8 1.5 multiply_reduce_fusion
  404.3 0.2 bitcast_multiply_fusion
  404.6 9.3 %all-gather = f32[8,4,2048]{2,1,0:T(4,128)S(1)} all-gather(f32[1,4,2048]{2,1,0:T(4,128)S(1)} %dynamic-slice_bitcast_fusion), channel_id=1, replica_groups=mesh['dp'=2,'tensor'=4,'fsdp'=4] {'dp','fsdp'}, dimensions={0}, use_global_device_ids=true | all-gather | bytes 294912 | tf_op jit(solution)/shard_map/all_gather | solution.py:62
  413.8 0.1 reshape.41
  413.9 0.3 fusion.8
  414.2 10.6 %psum.23 = f32[4,32]{1,0:T(4,128)S(1)} all-reduce(f32[4,32]{1,0:T(4,128)S(1)} %fusion.8), channel_id=1, replica_groups=mesh['dp'=2,'tensor'=4,'fsdp'=4] {'tensor'}, use_global_device_ids=true, to_apply=%region_3.4 | all-reduce | flops 128 | bytes 1024 | tf_op jit(solution)/shard_map/psum | solution.py:69
  424.8 0.6 broadcast_multiply_fusion
  (14 shorter events, 0.1 us)
Async XLA Ops:
  6.5 336.5 %copy-start = (bf16[2752,64]{0,1:T(8,128)(2,1)S(1)}, bf16[2752,64]{0,1:T(8,128)(2,1)}, u32[]{:S(2)}) copy-start(bf16[2752,64]{0,1:T(8,128)(2,1)} %param.18) | copy-start | bytes 1056772
  6.5 2.8 copy-start.2
  6.5 2.9 copy-start.1
  6.5 2.9 copy-start.3
  6.5 50.8 %all-gather.6.cloned.1.call-start = ((), (), s32[]{:S(2)}) async-start(), calls=%async_computation | async-start | bytes 2621440 | tf_op jit(solution)/shard_map/all_gather | solution.py:28
  7.3 96.1 %all-gather.8.cloned.1.call-start = ((), (), s32[]{:S(2)}) async-start(), calls=%async_computation.1 | async-start | bytes 2621440 | tf_op jit(solution)/shard_map/all_gather | solution.py:29
  8.0 214.7 %all-gather.10.cloned.1.call-start = ((), (), s32[]{:S(2)}) async-start(), calls=%async_computation.2 | async-start | bytes 25362432 | tf_op jit(solution)/shard_map/all_gather | solution.py:35
  8.8 334.3 %all-gather.12.cloned.1.call-start = ((), (), s32[]{:S(2)}) async-start(), calls=%async_computation.3 | async-start | bytes 25362432 | tf_op jit(solution)/shard_map/all_gather | solution.py:40
  9.3 393.4 %all-reduce.3.cloned.1.call-start = ((), (), s32[]{:S(2)}) async-start(), calls=%async_computation.4 | async-start | bytes 1048576 | tf_op jit(solution)/shard_map/psum | solution.py:48
  241.9 122.1 %copy-start.4 = (s32[4]{0:T(128)S(1)}, s32[4]{0:T(128)}, u32[]{:S(2)}) copy-start(s32[4]{0:T(128)} %param.15) | copy-start | bytes 52
  241.9 122.1 %copy-start.5 = (s32[4]{0:T(128)S(1)}, s32[4]{0:T(128)}, u32[]{:S(2)}) copy-start(s32[4]{0:T(128)} %param.14) | copy-start | bytes 52
Sparse Core Ops, SparseCore 0:
  8.9 48.3 all-gather.5
  58.9 44.4 all-gather.7
  105.3 117.3 all-gather.9
  224.4 118.5 all-gather.11
  364.1 38.6 all-reduce.2
where the time goes:
time: 432 us
  waiting for transfers between devices  348 us (81%)
  matrix products  42.2 us (10%)
  blocking collectives  19.9 us (5%)
  between operations  13.2 us (3%)
  local copies, waits for them, and re-layouts  7.28 us (2%)
    all_gather x1, waiting for transfers between devices, on_device(): lax.all_gather(gate_weight, ('dp', 'fsdp'), axis=0, tiled=True)  116 us
    all_gather x1, waiting for transfers between devices, on_device(): lax.all_gather(up_weight, ('dp', 'fsdp'), axis=0, tiled=True)  101 us
    all_gather x1, waiting for transfers between devices, on_device(): lax.all_gather(train_acts, 'tensor', axis=1, tiled=True)  46.8 us
    all_gather x1, waiting for transfers between devices, on_device(): lax.all_gather(val_acts, 'tensor', axis=1, tiled=True)  42.9 us
    psum x1, waiting for transfers between devices, on_device(): in_proj, out_proj = lax.psum((in_part, out_part), 'tensor')  38.7 us
    dot_general x1, matrix products, on_device(): in_part = jnp.dot(hidden, in_basis, preferred_element_type=jnp.float32)  20 us
    dot_general x1, matrix products, on_device(): jnp.dot(activations, lax.all_gather(gate_weight, ('dp', 'fsdp'), axis=0,...  19.2 us
    psum x1, blocking collectives, on_device(): product = lax.psum(partial_scores, 'tensor')  10.6 us
  transfers between devices with their start and end apart: 5, of which 5 were waited for; matrix products, arithmetic and copies ran while one was open for 6% of the time, Pallas kernels for 0%

commit v1 on v0

--- a/solution.py
+++ b/solution.py
@@ -1,9 +1,36 @@
+import functools
 import jax
 import jax.numpy as jnp
 from jax import lax
 from jax.sharding import PartitionSpec as P
 
 SEQ = 64
+
+
+def raise_series_all(here_x, dim_at):
+    here_x = jnp.moveaxis(here_x, 0, dim_at)
+    f_now = here_x.shape
+    prior = here_x.reshape(*f_now[:dim_at], f_now[dim_at] * f_now[dim_at + 1], *f_now[dim_at + 2 :])
+    return prior
+
+
+def derive_the_sectors(field, which_dim, axis_name):
+    n_chips = lax.psum(1, axis_name)
+    row_list = []
+    s = 0
+    while s < n_chips:
+        row_list.append((s, (s + 1) % n_chips))
+        s = s + 1
+    series = [field]
+    while len(series) < n_chips:
+        series.append(lax.ppermute(series[-1], axis_name, row_list))
+    piece_next = lax.axis_index(axis_name)
+    series = jnp.stack(series, axis=0)[(piece_next - jnp.arange(n_chips)) % n_chips]
+    part_now = raise_series_all(series, which_dim)
+    return part_now
+
+
+change_the_boxes = functools.partial(derive_the_sectors, which_dim=0, axis_name=("dp", "fsdp"))
 
 
 def outer_sums(in_proj, out_proj, valid):
@@ -35,11 +62,7 @@
         lax.all_gather(gate_weight, ("dp", "fsdp"), axis=0, tiled=True),
         preferred_element_type=jnp.float32,
     )
-    up_sum = jnp.dot(
-        activations,
-        lax.all_gather(up_weight, ("dp", "fsdp"), axis=0, tiled=True),
-        preferred_element_type=jnp.float32,
-    )
+    up_sum = jnp.dot(activations, change_the_boxes(up_weight), preferred_element_type=jnp.float32)
     hidden = (jax.nn.silu(gate_sum) * up_sum).astype(jnp.bfloat16)
     in_part = jnp.dot(hidden, in_basis, preferred_element_type=jnp.float32)
     out_part = jnp.dot(cotangents, out_basis, preferred_element_type=jnp.float32)

time: 432 us -> 540 us (1.25)
  local copies, waits for them, and re-layouts: 7.28 us -> 101 us
  other arithmetic: 0.9 us -> 24.3 us
  waiting for transfers between devices: 348 us -> 336 us
    ppermute x0 -> x7, waiting for transfers between devices: none -> 294 us  [derive_the_sectors(): series.append(lax.ppermute(series[-1], axis_name, row_list))]
    all_gather x1, waiting for transfers between devices: 116 us -> 0.01 us  [on_device(): lax.all_gather(gate_weight, ('dp', 'fsdp'), axis=0, tiled=True)]
    all_gather x1 -> x0, waiting for transfers between devices: 101 us -> none  [on_device(): lax.all_gather(up_weight, ('dp', 'fsdp'), axis=0, tiled=True)]
    unnamed x15 -> x21, local copies, waits for them, and re-layouts: 3.24 us -> 55.1 us
    all_gather x1, waiting for transfers between devices: 46.8 us -> 0.01 us  [on_device(): lax.all_gather(train_acts, 'tensor', axis=1, tiled=True)]
    all_gather x1, waiting for transfers between devices: 42.9 us -> 0.01 us  [on_device(): lax.all_gather(val_acts, 'tensor', axis=1, tiled=True)]
    gather x0 -> x4, local copies, waits for them, and re-layouts: none -> 40.2 us  [derive_the_sectors(): jnp.stack(series, axis=0)[(piece_next - jnp.arange(n_chips)) % n_chips]]
    unnamed x0 -> x1, other arithmetic: none -> 23.4 us
  transfers between devices with their start and end apart: 5 -> 11, of which waited for: 5 -> 8; matrix products, arithmetic and copies ran while one was open for 6% -> 23% of each run, Pallas kernels for 0% -> 0%
where the time goes in v1:
time: 540 us; the launch traced here: 539 us
  waiting for transfers between devices  336 us (62%)
  local copies, waits for them, and re-layouts  101 us (19%)
  matrix products  43.6 us (8%)
  other arithmetic  24.3 us (4%)
  blocking collectives  19.9 us (4%)
  between operations  13.2 us (2%)
    ppermute x7, waiting for transfers between devices, derive_the_sectors(): series.append(lax.ppermute(series[-1], axis_name, row_list))  294 us
    unnamed x21, local copies, waits for them, and re-layouts  55.1 us
    gather x4, local copies, waits for them, and re-layouts, derive_the_sectors(): jnp.stack(series, axis=0)[(piece_next - jnp.arange(n_chips)) % n_chips]  40.2 us
    psum x1, waiting for transfers between devices, on_device(): in_proj, out_proj = lax.psum((in_part, out_part), 'tensor')  39.4 us
    unnamed x1, other arithmetic  23.4 us
    dot_general x1, matrix products, on_device(): in_part = jnp.dot(hidden, in_basis, preferred_element_type=jnp.float32)  20.3 us
    dot_general x1, matrix products, on_device(): jnp.dot(activations, lax.all_gather(gate_weight, ('dp', 'fsdp'), axis=0,...  19 us
  transfers between devices with their start and end apart: 11, of which 8 were waited for; matrix products, arithmetic and copies ran while one was open for 23% of the time, Pallas kernels for 0%

profile of v1, /device:TPU:0, one launch (start us, length us, event | category | flops | bytes accessed | tf_op | source)
XLA Modules:
  0.0 538.7 jit_solution(12873274405071455922)
XLA Ops:
  6.5 0.7 all-gather.5.cloned.1.call-update
  9.3 34.5 %collective-permute-done = bf16[512,2752]{0,1:T(8,128)(2,1)S(1)} collective-permute-done((bf16[512,2752]{0,1:T(8,128)(2,1)}, bf16[512,2752]{0,1:T(8,128)(2,1)S(1)}, u32[]{:S(2)}, u32[]{:S(2)}) %collective-permute-start) | collective-permute-done | bytes 2818080 | tf_op jit(solution)/shard_map/ppermute | solution.py:26
  43.9 34.1 %collective-permute-done.1 = bf16[512,2752]{0,1:T(8,128)(2,1)S(1)} collective-permute-done((bf16[512,2752]{0,1:T(8,128)(2,1)S(1)}, bf16[512,2752]{0,1:T(8,128)(2,1)S(1)}, u32[]{:S(2)}, u32[]{:S(2)}) %collective-permute-start.1) | collective-permute-done | bytes 2818080 | tf_op jit(solution)/shard_map/ppermute | solution.py:26
  77.9 34.1 %collective-permute-done.2 = bf16[512,2752]{0,1:T(8,128)(2,1)S(1)} collective-permute-done((bf16[512,2752]{0,1:T(8,128)(2,1)S(1)}, bf16[512,2752]{0,1:T(8,128)(2,1)S(1)}, u32[]{:S(2)}, u32[]{:S(2)}) %collective-permute-start.2) | collective-permute-done | bytes 2818080 | tf_op jit(solution)/shard_map/ppermute | solution.py:26
  112.0 64.4 %collective-permute-done.3 = bf16[512,2752]{0,1:T(8,128)(2,1)} collective-permute-done((bf16[512,2752]{0,1:T(8,128)(2,1)S(1)}, bf16[512,2752]{0,1:T(8,128)(2,1)}, u32[]{:S(2)}, u32[]{:S(2)}) %collective-permute-start.3) | collective-permute-done | bytes 2818080 | tf_op jit(solution)/shard_map/ppermute | solution.py:26
  176.4 2.4 fusion
  178.9 3.5 bitcast_dynamic-update-slice_fusion.7
  182.4 78.0 %collective-permute-done.4 = bf16[512,2752]{0,1:T(8,128)(2,1)} collective-permute-done((bf16[512,2752]{0,1:T(8,128)(2,1)}, bf16[512,2752]{0,1:T(8,128)(2,1)}, u32[]{:S(2)}, u32[]{:S(2)}) %collective-permute-start.4) | collective-permute-done | bytes 2818080 | tf_op jit(solution)/shard_map/ppermute | solution.py:26
  260.5 3.5 bitcast_dynamic-update-slice_fusion.6
  264.0 3.2 constant_dynamic-update-slice_fusion.1
  267.2 3.2 constant_dynamic-update-slice_fusion
  270.3 3.6 bitcast_dynamic-update-slice_fusion.5
  273.9 27.5 %collective-permute-done.5 = bf16[512,2752]{0,1:T(8,128)(2,1)} collective-permute-done((bf16[512,2752]{0,1:T(8,128)(2,1)}, bf16[512,2752]{0,1:T(8,128)(2,1)}, u32[]{:S(2)}, u32[]{:S(2)}) %collective-permute-start.5) | collective-permute-done | bytes 2818080 | tf_op jit(solution)/shard_map/ppermute | solution.py:26
  301.4 1.8 bitcast_dynamic-update-slice_fusion.4
  303.2 3.6 bitcast_dynamic-update-slice_fusion.3
  306.8 3.5 bitcast_dynamic-update-slice_fusion.2
  310.3 3.5 bitcast_dynamic-update-slice_fusion.1
  313.9 21.8 %collective-permute-done.6 = bf16[512,2752]{0,1:T(8,128)(2,1)S(1)} collective-permute-done((bf16[512,2752]{0,1:T(8,128)(2,1)}, bf16[512,2752]{0,1:T(8,128)(2,1)S(1)}, u32[]{:S(2)}, u32[]{:S(2)}) %collective-permute-start.6) | collective-permute-done | bytes 2818080 | tf_op jit(solution)/shard_map/ppermute | solution.py:26
  335.7 1.8 bitcast_dynamic-update-slice_fusion
  337.5 9.8 %mini-gather-slice.2 = bf16[8,512,1408]{1,2,0:T(8,128)(2,1)} slice(bf16[8,512,2752]{1,2,0:T(8,128)(2,1)} %bitcast_dynamic-update-slice_fusion), slice={[0:8], [0:512], [0:1408]} | slice | bytes 23068672 | tf_op jit(solution)/shard_map/gather | solution.py:28
  347.3 10.1 %mini-gather-slice.3 = bf16[8,512,1344]{1,2,0:T(8,128)(2,1)} slice(bf16[8,512,2752]{1,2,0:T(8,128)(2,1)} %bitcast_dynamic-update-slice_fusion), slice={[0:8], [0:512], [1408:2752]} | slice | bytes 22020096 | tf_op jit(solution)/shard_map/gather | solution.py:28
  357.4 10.4 %gather_fusion = bf16[8,512,1408]{1,2,0:T(8,128)(2,1)} fusion(bf16[8,512,1408]{1,2,0:T(8,128)(2,1)} %mini-gather-slice.2, s32[1024]{0:T(1024)S(1)} %pad_clamp_fusion), kind=kCustom, calls=%fused_computation | custom fusion | bytes 23068704 | tf_op jit(solution)/shard_map/gather | solution.py:28
  367.7 9.9 %gather_fusion.1 = bf16[8,512,1344]{1,2,0:T(8,128)(2,1)} fusion(bf16[8,512,1344]{1,2,0:T(8,128)(2,1)} %mini-gather-slice.3, s32[1024]{0:T(1024)S(1)} %pad_clamp_fusion), kind=kCustom, calls=%fused_computation.1 | custom fusion | bytes 22020128 | tf_op jit(solution)/shard_map/gather | solution.py:28
  377.6 23.4 %pad_maximum_fusion = bf16[8,512,2752]{1,2,0:T(8,128)(2,1)} fusion(bf16[8,512,1344]{1,2,0:T(8,128)(2,1)} %gather_fusion.1, bf16[8,512,1408]{1,2,0:T(8,128)(2,1)} %gather_fusion), kind=kLoop, calls=%fused_computation.2 | loop fusion | flops 45088768 | bytes 45088768
  401.0 28.7 %copy.14 = bf16[8,512,2752]{2,1,0:T(8,128)(2,1)} copy(bf16[8,512,2752]{1,2,0:T(8,128)(2,1)} %pad_maximum_fusion) | data formatting | bytes 45088768
  429.7 19.0 %fusion.15 = f32[512,2752]{0,1:T(8,128)} fusion(bf16[512,4096]{1,0:T(8,128)(2,1)} %constant_dynamic-update-slice_fusion, bf16[4096,2752]{0,1:T(8,128)(2,1)} %all-gather.9.cloned.1.call-done), kind=kOutput, calls=%fused_computation.41 | convolution fusion | flops 11542724608 | bytes 32374784 | tf_op jit(solution)/shard_map/dot_general | solution.py:60
  448.7 20.3 %fusion.16 = f32[512,64]{0,1:T(8,128)S(1)} fusion(bf16[2752,64]{0,1:T(8,128)(2,1)S(1)} %copy-done, f32[512,2752]{0,1:T(8,128)} %fusion.15, bf16[512,4096]{1,0:T(8,128)(2,1)} %constant_dynamic-update-slice_fusion, bf16[4096,2752]{1,0:T(8,128)(2,1)} %bitcast.44), kind=kOutput, calls=%fused_computation.42 | convolution fusion | flops 11731533824 | bytes 32858112 | tf_op jit(solution)/shard_map/dot_general | solution.py:67
  469.2 0.7 copy.15
  470.1 39.4 %all-reduce.3.cloned.1.call-done = (f32[8,64,128]{2,1,0:T(8,128)}, f32[8,64,64]{1,2,0:T(8,128)}) async-done(((f32[8,64,128]{2,1,0:T(8,128)}, f32[8,64,64]{1,2,0:T(8,128)}), (f32[8,64,128]{2,1,0:T(8,128)}, f32[8,64,64]{1,2,0:T(8,128)})) %all-reduce.3.cloned.1.call-update) | async-done | bytes 393232 | tf_op jit(solution)/shard_map/psum | solution.py:71
  509.5 1.5 multiply_reduce_fusion
  511.3 9.3 %all-gather = f32[8,4,2048]{2,1,0:T(4,128)S(1)} all-gather(f32[1,4,2048]{2,1,0:T(4,128)S(1)} %dynamic-slice_bitcast_fusion), channel_id=1, replica_groups=mesh['dp'=2,'tensor'=4,'fsdp'=4] {'dp','fsdp'}, dimensions={0}, use_global_device_ids=true | all-gather | bytes 294912 | tf_op jit(solution)/shard_map/all_gather | solution.py:85
  520.9 10.6 %psum.23 = f32[4,32]{1,0:T(4,128)S(1)} all-reduce(f32[4,32]{1,0:T(4,128)S(1)} %fusion.7), channel_id=1, replica_groups=mesh['dp'=2,'tensor'=4,'fsdp'=4] {'tensor'}, use_global_device_ids=true, to_apply=%region_3.4 | all-reduce | flops 128 | bytes 1024 | tf_op jit(solution)/shard_map/psum | solution.py:92
  (39 shorter events, 3.5 us)
Async XLA Ops:
  6.5 442.2 %copy-start = (bf16[2752,64]{0,1:T(8,128)(2,1)S(1)}, bf16[2752,64]{0,1:T(8,128)(2,1)}, u32[]{:S(2)}) copy-start(bf16[2752,64]{0,1:T(8,128)(2,1)} %param.18) | copy-start | bytes 1056772
  6.5 257.5 %all-gather.5.cloned.1.call-start = ((), (), s32[]{:S(2)}) async-start(), calls=%async_computation | async-start | bytes 2621440 | tf_op jit(solution)/shard_map/all_gather | solution.py:55
  7.3 259.9 %all-gather.7.cloned.1.call-start = ((), (), s32[]{:S(2)}) async-start(), calls=%async_computation.1 | async-start | bytes 2621440 | tf_op jit(solution)/shard_map/all_gather | solution.py:56
  8.0 421.7 %all-gather.9.cloned.1.call-start = ((), (), s32[]{:S(2)}) async-start(), calls=%async_computation.2 | async-start | bytes 25362432 | tf_op jit(solution)/shard_map/all_gather | solution.py:62
  8.7 500.8 %all-reduce.3.cloned.1.call-start = ((), (), s32[]{:S(2)}) async-start(), calls=%async_computation.3 | async-start | bytes 1048576 | tf_op jit(solution)/shard_map/psum | solution.py:71
  8.8 35.1 %collective-permute-start = (bf16[512,2752]{0,1:T(8,128)(2,1)}, bf16[512,2752]{0,1:T(8,128)(2,1)S(1)}, u32[]{:S(2)}, u32[]{:S(2)}) collective-permute-start(bf16[512,2752]{0,1:T(8,128)(2,1)} %param.17), channel_id=1, source_target_pairs={{0,1},{1,2},{2,3},{3,16},{16,17},{17,18},{18,19},{19,0},{4,5},{5,6... | collective-permute-start | bytes 8454152 | tf_op jit(solution)/shard_map/ppermute | solution.py:26
  43.9 132.6 %copy-start.2 = (bf16[512,2752]{0,1:T(8,128)(2,1)}, bf16[512,2752]{0,1:T(8,128)(2,1)S(1)}, u32[]{:S(2)}) copy-start(bf16[512,2752]{0,1:T(8,128)(2,1)S(1)} %collective-permute-done) | copy-start | bytes 8454148
  43.9 34.1 %collective-permute-start.1 = (bf16[512,2752]{0,1:T(8,128)(2,1)S(1)}, bf16[512,2752]{0,1:T(8,128)(2,1)S(1)}, u32[]{:S(2)}, u32[]{:S(2)}) collective-permute-start(bf16[512,2752]{0,1:T(8,128)(2,1)S(1)} %collective-permute-done), channel_id=1, source_target_pairs={{0,1},{1,2},{2,3},{3,16},{16,17},{17,18},{18,19},{19,0},{4,5},{5,6... | collective-permute-start | bytes 8454152 | tf_op jit(solution)/shard_map/ppermute | solution.py:26
  77.9 98.5 %copy-start.1 = (bf16[512,2752]{0,1:T(8,128)(2,1)}, bf16[512,2752]{0,1:T(8,128)(2,1)S(1)}, u32[]{:S(2)}) copy-start(bf16[512,2752]{0,1:T(8,128)(2,1)S(1)} %collective-permute-done.1) | copy-start | bytes 8454148
  77.9 34.1 %collective-permute-start.2 = (bf16[512,2752]{0,1:T(8,128)(2,1)S(1)}, bf16[512,2752]{0,1:T(8,128)(2,1)S(1)}, u32[]{:S(2)}, u32[]{:S(2)}) collective-permute-start(bf16[512,2752]{0,1:T(8,128)(2,1)S(1)} %collective-permute-done.1), channel_id=1, source_target_pairs={{0,1},{1,2},{2,3},{3,16},{16,17},{17,18},{18,19},{19,0},{4,5},{5,6... | collective-permute-start | bytes 8454152 | tf_op jit(solution)/shard_map/ppermute | solution.py:26
  112.0 64.4 %collective-permute-start.3 = (bf16[512,2752]{0,1:T(8,128)(2,1)S(1)}, bf16[512,2752]{0,1:T(8,128)(2,1)}, u32[]{:S(2)}, u32[]{:S(2)}) collective-permute-start(bf16[512,2752]{0,1:T(8,128)(2,1)S(1)} %collective-permute-done.2), channel_id=1, source_target_pairs={{0,1},{1,2},{2,3},{3,16},{16,17},{17,18},{18,19},{19,0},{4,5},{5,6... | collective-permute-start | bytes 8454152 | tf_op jit(solution)/shard_map/ppermute | solution.py:26
  176.4 84.0 %collective-permute-start.4 = (bf16[512,2752]{0,1:T(8,128)(2,1)}, bf16[512,2752]{0,1:T(8,128)(2,1)}, u32[]{:S(2)}, u32[]{:S(2)}) collective-permute-start(bf16[512,2752]{0,1:T(8,128)(2,1)} %collective-permute-done.3), channel_id=1, source_target_pairs={{0,1},{1,2},{2,3},{3,16},{16,17},{17,18},{18,19},{19,0},{4,5},{5,6... | collective-permute-start | bytes 8454152 | tf_op jit(solution)/shard_map/ppermute | solution.py:26
  260.4 41.0 %collective-permute-start.5 = (bf16[512,2752]{0,1:T(8,128)(2,1)}, bf16[512,2752]{0,1:T(8,128)(2,1)}, u32[]{:S(2)}, u32[]{:S(2)}) collective-permute-start(bf16[512,2752]{0,1:T(8,128)(2,1)} %collective-permute-done.4), channel_id=1, source_target_pairs={{0,1},{1,2},{2,3},{3,16},{16,17},{17,18},{18,19},{19,0},{4,5},{5,6... | collective-permute-start | bytes 8454152 | tf_op jit(solution)/shard_map/ppermute | solution.py:26
  301.4 34.3 %collective-permute-start.6 = (bf16[512,2752]{0,1:T(8,128)(2,1)}, bf16[512,2752]{0,1:T(8,128)(2,1)S(1)}, u32[]{:S(2)}, u32[]{:S(2)}) collective-permute-start(bf16[512,2752]{0,1:T(8,128)(2,1)} %collective-permute-done.5), channel_id=1, source_target_pairs={{0,1},{1,2},{2,3},{3,16},{16,17},{17,18},{18,19},{19,0},{4,5},{5,6... | collective-permute-start | bytes 8454152 | tf_op jit(solution)/shard_map/ppermute | solution.py:26
  448.7 21.2 %copy-start.3 = (s32[4]{0:T(128)S(1)}, s32[4]{0:T(128)}, u32[]{:S(2)}) copy-start(s32[4]{0:T(128)} %param.15) | copy-start | bytes 52
  448.7 21.2 %copy-start.4 = (s32[4]{0:T(128)S(1)}, s32[4]{0:T(128)}, u32[]{:S(2)}) copy-start(s32[4]{0:T(128)} %param.14) | copy-start | bytes 52
Sparse Core Ops, SparseCore 0:
  8.9 48.3 all-gather.4
  58.9 44.4 all-gather.6
  105.3 176.5 all-gather.8
  470.0 39.4 all-reduce.2
